TPU v7x, 32 devices: a whole 2x2x4 slice. The times are simulated.
32 devices in a mesh: py: 4 (over y, x), px: 8 (over z, core).
Axes of the slice: x: 2, y: 2, z: 4, core: 2. Of those that a mesh axis runs over, the one named last changes fastest.
Arguments:
- movie: bfloat16 [256, 128, 2048], P('py', 'px'), may hold values from -6 to 6
- traces: bfloat16 [4096, 2048], P('py', 'px'), may hold values from -0.125 to 0.125
- footprints: float32 [256, 128, 512], P('py', 'px'), may hold values from 0 to 1
- block_ids: int32 [4, 8, 4], P('py', 'px'), may hold values from 0 to 32, as said below
Outputs:
- updated: float32 [256, 128, 512], P('py', 'px')
Inputs may be any that keep to these rules, and one draw needn't show every extreme that they name: `block_ids`: in each tile's list of 4 entries the live entries come first and are distinct block numbers below 32; the remaining entries equal 32 and mark empty slots. Every tile has at least one live entry, and some tile has all 4 live.
All inputs are finite; a program needn't handle non-finite values.
Results may differ from a plain program's by a relative error of at most 0.0003.
Values may be sent and summed in bfloat16 or wider, within the bound.
A program may use at most 64 MiB of HBM per device.

v0:
```python
import jax
import jax.numpy as jnp
from jax import lax
from jax.sharding import PartitionSpec as P

K = 4096
BLK = 128
SLOTS = 4
ITERS = 2


def accumulate(tile_movie, picked):
    cross = lax.dot_general(
        tile_movie, picked, (((1,), (1,)), ((), ())), preferred_element_type=jnp.float32
    )
    gram = lax.dot_general(
        picked, picked, (((1,), (1,)), ((), ())), preferred_element_type=jnp.float32
    )
    return (cross, gram)


def per_device(movie, traces, footprints, block_ids):
    rows, cols, frames = movie.shape
    pixels = rows * cols
    width = SLOTS * BLK
    nblk = K // BLK
    tile_movie = movie.reshape(pixels, frames)
    ids = block_ids.reshape(SLOTS)
    onehot = (ids[:, None] == jnp.arange(nblk, dtype=jnp.int32)[None, :]).astype(jnp.float32)
    live = jnp.sum(onehot, axis=1)
    span_all = lax.all_gather(traces, "py", axis=0, tiled=True)
    span_len = span_all.shape[1]
    row_ids = lax.all_gather(block_ids, "px", axis=1, tiled=True).reshape(-1, SLOTS)
    route = (row_ids[:, :, None] == jnp.arange(nblk, dtype=jnp.int32)[None, None, :]).astype(
        jnp.bfloat16
    )
    outgoing = jnp.einsum(
        "rsb,bnw->rsnw",
        route,
        span_all.reshape(nblk, BLK, span_len),
        preferred_element_type=jnp.float32,
    )
    outgoing = outgoing.astype(jnp.bfloat16).reshape(row_ids.shape[0], width, span_len)
    received = lax.all_to_all(outgoing, "px", split_axis=0, concat_axis=2, tiled=True)
    mine = received.reshape(width, frames)
    cross, gram = accumulate(tile_movie, mine)
    column_live = jnp.repeat(live, BLK)
    denom = jnp.diagonal(gram) + 1e-06 + (1.0 - column_live)
    current = footprints.reshape(pixels, width) * column_live[None, :]
    pixall = pixels * lax.axis_size("py") * lax.axis_size("px")
    for step in range(ITERS):
        for slot in range(SLOTS):
            low = slot * BLK
            resid = cross[:, low : low + BLK] - jnp.dot(
                current, gram[:, low : low + BLK], precision=lax.Precision.HIGHEST
            )
            fresh = jnp.maximum(
                current[:, low : low + BLK] + resid / denom[None, low : low + BLK], 0.0
            )
            current = current.at[:, low : low + BLK].set(fresh)
        colsq = jnp.sum(current * current, axis=0).reshape(SLOTS, BLK)
        partial_value = jnp.einsum("sb,sn->bn", onehot, colsq, precision=lax.Precision.HIGHEST)
        totals = lax.psum(partial_value, ("py", "px"))
        factor = 1.0 / jnp.sqrt(totals / pixall + 1e-06)
        scale = jnp.einsum("sb,bn->sn", onehot, factor, precision=lax.Precision.HIGHEST).reshape(
            width
        )
        current = current * scale[None, :]
    return current.reshape(rows, cols, width)


def solution(mesh):
    return jax.shard_map(
        per_device,
        mesh=mesh,
        in_specs=(P("py", "px", None), P("py", "px"), P("py", "px", None), P("py", "px", None)),
        out_specs=P("py", "px", None),
        check_vma=False,
    )
```

profile of v0, /device:TPU:0, one launch (start us, length us, event | category | flops | bytes accessed | tf_op | source)
XLA Modules:
  0.0 233.0 jit_solution(12457084238456742489)
XLA Ops:
  6.5 0.0 all-gather.2.cloned.1.call-start
  6.5 0.7 all-gather.2.cloned.1.call-update
  7.3 13.6 %all_gather.6 = s32[1,8,4]{2,0,1:T(1,128)S(1)} all-gather(s32[1,1,4]{2,0,1:T(1,128)} %bitcast.62), channel_id=1, replica_groups=mesh['py'=4,'px'=8] {'px'}, dimensions={1}, use_global_device_ids=true | all-gather | bytes 144 | tf_op jit(solution)/shard_map/all_gather | solution.py:33
  20.9 0.1 copy.48
  21.0 26.1 %all-gather.2.cloned.1.call-done = bf16[4096,256]{1,0:T(8,128)(2,1)} async-done(((bf16[1024,256]{1,0:T(8,128)(2,1)}), bf16[4096,256]{1,0:T(8,128)(2,1)}) %all-gather.2.cloned.1.call-update) | async-done | bytes 2097168 | tf_op jit(solution)/shard_map/all_gather | solution.py:31
  47.1 2.9 %fusion.5 = bf16[8,4,128,256]{3,0,2,1:T(8,128)(2,1)S(1)} fusion(bf16[32,128,256]{2,1,0:T(8,128)(2,1)} %bitcast.60, s32[8,4]{0,1:T(4,128)S(1)} %bitcast.61), kind=kOutput, calls=%fused_computation.8 | convolution fusion | flops 68158464 | bytes 4194432 | tf_op jit(solution)/shard_map/rsb,bnw->rsnw/dot_general | solution.py:37
  50.0 1.7 copy.50
  51.7 0.0 copy-start.3
  51.8 4.7 %all-to-all-start = ((bf16[8,512,256]{2,1,0:T(8,128)(2,1)}), bf16[8,512,256]{2,1,0:T(8,128)(2,1)}, u32[]{:S(2)}, u32[]{:S(2)}) async-start(bf16[8,512,256]{2,1,0:T(8,128)(2,1)} %copy.50), calls=%async_computation | async-start | bytes 4194304 | tf_op jit(solution)/shard_map/all_to_all | solution.py:44
  56.5 0.0 copy-done.3
  56.5 0.0 copy-start.4
  56.5 1.8 copy.46
  58.3 0.6 compare_reduce_fusion.2
  59.0 0.7 compare_reduce_fusion
  59.7 0.0 copy-done.4
  59.7 0.2 convert_reduce_fusion
  59.9 0.1 broadcast_bitcast_fusion
  60.0 1.8 broadcast_multiply_fusion.2
  61.8 43.9 %all-to-all-done = bf16[8,512,256]{2,1,0:T(8,128)(2,1)} async-done(((bf16[8,512,256]{2,1,0:T(8,128)(2,1)}), bf16[8,512,256]{2,1,0:T(8,128)(2,1)}, u32[]{:S(2)}, u32[]{:S(2)}) %all-to-all-start) | async-done | bytes 2097184 | tf_op jit(solution)/shard_map/all_to_all | solution.py:44
  105.6 3.5 %fusion.8 = f32[512,512]{1,0:T(8,128)S(1)} fusion(bf16[8,512,256]{2,1,0:T(8,128)(2,1)} %all-to-all-done), kind=kOutput, calls=%fused_computation.10 | convolution fusion | flops 1073741824 | bytes 3145728 | tf_op jit(solution)/shard_map/dot_general | solution.py:16
  109.1 4.5 %gather_fusion = f32[512]{0:T(512)S(1)} fusion(f32[512,512]{1,0:T(8,128)S(1)} %fusion.8, s32[512]{0:T(512)S(1)} %bitcast.56), kind=kCustom, calls=%fused_computation | custom fusion | bytes 8192 | tf_op jit(solution)/shard_map/jit(diagonal)/cond/branch_0_fun/gather | solution.py:48
  113.7 0.1 subtract_add_fusion
  113.7 3.9 %copy.51 = bf16[1,512,8,256]{1,3,2,0:T(8,128)(2,1)} copy(bf16[1,512,8,256]{3,1,2,0:T(8,128)(2,1)} %bitcast.11) | data formatting | bytes 4194304 | tf_op jit(solution)/shard_map/all_to_all | solution.py:44
  117.7 5.2 %convolution_bitcast_fusion = f32[1024,512]{0,1:T(8,128)S(1)} fusion(bf16[512,2048]{0,1:T(8,128)(2,1)} %bitcast.59, bf16[1024,2048]{1,0:T(8,128)(2,1)} %bitcast.68), kind=kOutput, calls=%fused_computation.9 | convolution fusion | flops 2147483648 | bytes 8388608 | tf_op jit(solution)/shard_map/dot_general | solution.py:13
  122.9 0.0 copy-start.1
  122.9 2.1 fusion.40
  125.0 2.2 fusion.36
  127.2 2.1 fusion.32
  129.3 0.0 copy-done.1
  129.4 1.5 fusion.28
  130.9 0.2 multiply_reduce_fusion.1
  131.1 0.3 fusion.64
  131.3 37.2 %psum.14 = f32[32,128]{1,0:T(8,128)S(1)} all-reduce(f32[32,128]{1,0:T(8,128)S(1)} %fusion.64), channel_id=1, replica_groups=mesh['py'=4,'px'=8] {'py','px'}, use_global_device_ids=true, to_apply=%region_5.6 | all-reduce | flops 4096 | bytes 32768 | tf_op jit(solution)/shard_map/psum | solution.py:63
  168.5 0.2 convolution_bitcast_fusion.2
  168.7 0.2 broadcast_multiply_fusion.1
  168.9 1.4 copy-done.2
  170.3 2.1 fusion.25
  172.4 2.1 fusion.21
  174.6 2.0 fusion.17
  176.7 1.4 fusion.13
  178.1 0.0 copy-start
  178.2 1.3 copy-done
  179.5 0.2 multiply_reduce_fusion
  179.7 0.3 fusion.62
  179.9 42.4 %psum.15 = f32[32,128]{1,0:T(8,128)S(1)} all-reduce(f32[32,128]{1,0:T(8,128)S(1)} %fusion.62), channel_id=1, replica_groups=mesh['py'=4,'px'=8] {'py','px'}, use_global_device_ids=true, to_apply=%region_7.8 | all-reduce | flops 4096 | bytes 32768 | tf_op jit(solution)/shard_map/psum | solution.py:63
  222.3 0.2 convolution_bitcast_fusion.1
  222.5 1.8 broadcast_multiply_fusion
  224.3 1.8 copy.60
  (11 shorter events, 0.3 us)
Async XLA Ops:
  6.5 40.6 %all-gather.2.cloned.1.call-start = ((), (), s32[]{:S(2)}) async-start(), calls=%async_computation.1 | async-start | bytes 2621440 | tf_op jit(solution)/shard_map/all_gather | solution.py:31
  51.7 4.7 %copy-start.3 = (f32[64,16,512]{2,1,0:T(8,128)S(1)}, f32[64,16,512]{2,1,0:T(8,128)}, u32[]{:S(2)}) copy-start(f32[64,16,512]{2,1,0:T(8,128)} %param.22) | copy-start | bytes 6291460
  51.8 53.9 %all-to-all-start = ((bf16[8,512,256]{2,1,0:T(8,128)(2,1)}), bf16[8,512,256]{2,1,0:T(8,128)(2,1)}, u32[]{:S(2)}, u32[]{:S(2)}) async-start(bf16[8,512,256]{2,1,0:T(8,128)(2,1)} %copy.50), calls=%async_computation | async-start | bytes 4194304 | tf_op jit(solution)/shard_map/all_to_all | solution.py:44
  56.5 3.2 %copy-start.4 = (s32[1,1,4]{2,1,0:T(1,128)S(1)}, s32[1,1,4]{2,1,0:T(1,128)}, u32[]{:S(2)}) copy-start(s32[1,1,4]{2,1,0:T(1,128)} %param.23) | copy-start | bytes 52
  122.9 6.5 %copy-start.1 = (f32[1024,512]{0,1:T(8,128)}, f32[1024,512]{0,1:T(8,128)S(1)}, u32[]{:S(2)}) copy-start(f32[1024,512]{0,1:T(8,128)S(1)} %convolution_bitcast_fusion) | copy-start | bytes 6291460
  168.7 1.6 copy-start.2
  178.1 1.3 copy-start
Sparse Core Ops, SparseCore 0:
  9.2 37.8 all-gather.1
where the time goes:
time: 234 us; the launch traced here: 233 us
  blocking collectives  93.2 us (40%)
  waiting for transfers between devices  70.7 us (30%)
  matrix products  27.9 us (12%)
  local copies, waits for them, and re-layouts  17 us (7%)
  between operations  13.6 us (6%)
  other arithmetic  5.86 us (3%)
  starting transfers between devices  4.74 us (2%)
    psum x2, blocking collectives, per_device(): totals = lax.psum(partial_value, ('py', 'px'))  79.5 us
    all_to_all x1, waiting for transfers between devices, per_device(): lax.all_to_all(outgoing, 'px', split_axis=0, concat_axis=2, tiled=True)  43.9 us
    all_gather x1, waiting for transfers between devices, per_device(): span_all = lax.all_gather(traces, 'py', axis=0, tiled=True)  26.1 us
    dot_general x8, matrix products, per_device(): jnp.dot(current, gram[:, low:low + BLK], precision=lax.Precision.HIGHEST)  15.4 us
    all_gather x1, blocking collectives, per_device(): lax.all_gather(block_ids, 'px', axis=1, tiled=True).reshape(-1, SLOTS)  13.6 us
    dot_general x1, matrix products, accumulate(): lax.dot_general(tile_movie, picked, (((1,), (1,)), ((), ())), preferred_e...  5.2 us
    all_to_all x1, starting transfers between devices, per_device(): lax.all_to_all(outgoing, 'px', split_axis=0, concat_axis=2, tiled=True)  4.74 us
  transfers between devices with their start and end apart: 2, of which 2 were waited for; matrix products, arithmetic and copies ran while one was open for 2% of the time, Pallas kernels for 0%

commit v1 on v0

v1 whole, which is shorter than its diff:
```python
import functools

import jax
import jax.numpy as jnp
from jax import lax
from jax.experimental import pallas as pl
from jax.experimental.pallas import tpu as pltpu
from jax.sharding import PartitionSpec as P

ITERS = 2
CHUNKS = 4
MESH = pl.DeviceIdType.MESH
BF = jnp.bfloat16
F32 = jnp.float32


def split(x):
    hi = x.astype(BF)
    return hi, (x - hi.astype(F32)).astype(BF)


def mm(a, b):
    return lax.dot_general(a, b, (((1,), (0,)), ((), ())), preferred_element_type=F32)


def kernel(
    n_py, n_px, movie, traces, foot, ids, cur_out, scale_out,
    y_buf, outb, recv, land, cur, crs, hilo, id_tile, id_all, id_smem, t_send, t_recv, live_row,
    local_sem, own_sem, id_ssem, id_rsem, g_ssem, g_rsem, x_ssem, x_rsem, t_ssem, t_rsem, *spans,
):
    py, px = lax.axis_index("py"), lax.axis_index("px")
    total = n_py * n_px
    me = py * n_px + px
    loc, blk, wid = traces.shape
    nblk = loc * n_py
    slots = recv.shape[0]
    width = slots * blk
    direct = wid % 128 == 0
    pixels = y_buf.shape[0]
    step_rows = blk // CHUNKS

    owns = [
        pltpu.make_async_copy(
            traces.at[:, pl.ds(c * step_rows, step_rows), :], spans[c].at[pl.ds(py * loc, loc)], own_sem.at[c]
        )
        for c in range(CHUNKS)
    ]
    for own in owns:
        own.start()
    get_foot = pltpu.make_async_copy(foot, cur, local_sem.at[1])
    get_movie = pltpu.make_async_copy(movie, y_buf, local_sem.at[2])

    sub = lax.broadcasted_iota(jnp.int32, (8, blk), 0)
    tile = jnp.zeros((8, blk), jnp.int32)
    for s in range(slots):
        tile = jnp.where(sub == 4 + s, ids[0, 0, s], tile)
    id_tile[...] = tile
    id_all[px] = tile
    for s in range(slots):
        alive = ((tile[4 + s : 5 + s, :] >= 0) & (tile[4 + s : 5 + s, :] < nblk)).astype(F32)
        live_row[:, s * blk : (s + 1) * blk] = alive

    barrier = pltpu.get_barrier_semaphore()

    def greet(k, _):
        dest = lax.rem(me + k, total)
        pl.semaphore_signal(
            barrier, inc=1, device_id={"py": dest // n_px, "px": lax.rem(dest, n_px)}, device_id_type=MESH
        )
        return _

    lax.fori_loop(1, total, greet, 0)
    pl.semaphore_wait(barrier, total - 1)

    def id_copy(k):
        return pltpu.make_async_remote_copy(
            src_ref=id_tile, dst_ref=id_all.at[px], send_sem=id_ssem.at[k], recv_sem=id_rsem.at[k],
            device_id={"px": lax.rem(px + k, n_px)}, device_id_type=MESH,
        )

    def gather_copy(c, k):
        rows = pl.ds(c * step_rows, step_rows)
        return pltpu.make_async_remote_copy(
            src_ref=traces.at[:, rows, :], dst_ref=spans[c].at[pl.ds(py * loc, loc)],
            send_sem=g_ssem.at[c, k], recv_sem=g_rsem.at[c, k],
            device_id={"py": lax.rem(py + k, n_py)}, device_id_type=MESH,
        )

    def x_copy(c, k):
        rows = pl.ds(c * step_rows, step_rows)
        dest = lax.rem(px + k, n_px)
        if direct:
            target = recv.at[:, rows, pl.ds(pl.multiple_of(px * wid, wid), wid)]
        else:
            target = land.at[px, :, rows, :]
        return pltpu.make_async_remote_copy(
            src_ref=outb.at[dest, :, rows, :],
            dst_ref=target,
            send_sem=x_ssem.at[c, k], recv_sem=x_rsem.at[c, k],
            device_id={"px": dest}, device_id_type=MESH,
        )

    def run(lo, hi, fn):
        def body(k, carry):
            fn(k)
            return carry

        lax.fori_loop(lo, hi, body, 0)

    run(1, n_px, lambda k: id_copy(k).start())
    for c in range(CHUNKS):
        run(1, n_py, lambda k: gather_copy(c, k).start())
    get_movie.start()
    get_foot.start()
    run(1, n_px, lambda k: id_copy(k).wait())
    to_smem = pltpu.make_async_copy(id_all, id_smem, local_sem.at[3])
    to_smem.start()
    to_smem.wait()

    def pick(dest, s, c):
        number = id_smem[dest, 4 + s, 0]
        ok = ((number >= 0) & (number < nblk)).astype(F32).astype(BF)
        index = jnp.minimum(jnp.maximum(number, 0), nblk - 1)
        return spans[c][index] * ok

    for c in range(CHUNKS):
        rows = pl.ds(c * step_rows, step_rows)
        owns[c].wait()
        run(1, n_py, lambda k: gather_copy(c, k).wait_recv())

        def route(k):
            dest = lax.rem(px + k, n_px)
            for s in range(slots):
                outb[dest, s, rows, :] = pick(dest, s, c)
            x_copy(c, k).start()

        run(1, n_px, route)
        for s in range(slots):
            if direct:
                recv[s, rows, pl.ds(pl.multiple_of(px * wid, wid), wid)] = pick(px, s, c)
            else:
                land[px, s, rows, :] = pick(px, s, c)

    get_foot.wait()
    get_movie.wait()
    for c in range(CHUNKS):
        run(1, n_px, lambda k: x_copy(c, k).wait_recv())
    if not direct:
        pack = blk // wid
        for q in range(n_px // pack):
            both = [land[q * pack + j] for j in range(pack)]
            recv[:, :, q * blk : (q + 1) * blk] = jnp.concatenate(both, axis=-1)

    mine = recv[...].reshape(width, recv.shape[2])
    gram = lax.dot_general(mine, mine, (((1,), (1,)), ((), ())), preferred_element_type=F32)
    eye = lax.broadcasted_iota(jnp.int32, (width, width), 0) == lax.broadcasted_iota(jnp.int32, (width, width), 1)
    live = live_row[...]
    denom = jnp.sum(jnp.where(eye, gram, 0.0), axis=0, keepdims=True) + 1e-06 + (1.0 - live)
    inv = 1.0 / denom
    hi, lo = split(jnp.where(eye, 1.0, 0.0) - gram * inv)
    for s in range(slots):
        hilo[s, :, :blk] = hi[:, s * blk : (s + 1) * blk]
        hilo[s, :, blk:] = lo[:, s * blk : (s + 1) * blk]
    part = min(pixels, 256)

    def cross_part(i):
        at = pl.ds(pl.multiple_of(i * part, part), part)
        prod = lax.dot_general(
            y_buf[at, :], recv[...].reshape(width, recv.shape[2]), (((1,), (1,)), ((), ())), preferred_element_type=F32
        )
        crs[at, :] = prod * inv
        cur[at, :] = cur[at, :] * live

    run(0, pixels // part, cross_part)

    def total_copy(step, k):
        dest = lax.rem(me + k, total)
        return pltpu.make_async_remote_copy(
            src_ref=t_send.at[step], dst_ref=t_recv.at[step, k - 1],
            send_sem=t_ssem.at[step], recv_sem=t_rsem.at[step],
            device_id={"py": dest // n_px, "px": lax.rem(dest, n_px)}, device_id_type=MESH,
        )

    ids_f = tile.astype(F32)
    scale = jnp.ones((1, width), F32)
    put = pltpu.make_async_copy(cur, cur_out, local_sem.at[4])
    for step in range(ITERS):

        def sweep(i, sums, scale=scale):
            at = pl.ds(pl.multiple_of(i * part, part), part)
            now = cur[at, :] * scale
            pieces = [now[:, s * blk : (s + 1) * blk] for s in range(slots)]
            his, los = zip(*[split(p) for p in pieces])
            his, los = list(his), list(los)
            squares = []
            for s in range(slots):
                m = hilo[s]
                wide = mm(jnp.concatenate(his, axis=1), m)
                thin = mm(jnp.concatenate(los, axis=1), m[:, :blk])
                fresh = jnp.maximum(
                    crs[at, s * blk : (s + 1) * blk] + (wide[:, :blk] + wide[:, blk:] + thin), 0.0
                )
                cur[at, s * blk : (s + 1) * blk] = fresh
                his[s], los[s] = split(fresh)
                squares.append(jnp.sum(fresh * fresh, axis=0, keepdims=True))
            return sums + jnp.concatenate(squares, axis=1)

        sums = lax.fori_loop(0, pixels // part, sweep, jnp.zeros((1, width), F32))
        mine_tile = ids_f
        for s in range(slots):
            mine_tile = jnp.where(sub == s, sums[:, s * blk : (s + 1) * blk], mine_tile)
        t_send[step] = mine_tile
        run(1, total, lambda k: total_copy(step, k).start())
        if step == ITERS - 1:
            put.start()
        pltpu.make_async_copy(t_recv.at[step], t_recv.at[step], t_rsem.at[step]).wait()
        got = t_recv[step]
        scales = []
        for s in range(slots):
            want = ids_f[4 + s : 5 + s, :]
            acc = sums[:, s * blk : (s + 1) * blk]
            same = jnp.where(got[:, 4 : 4 + slots, :] == want[None], got[:, :slots, :], 0.0)
            acc = acc + jnp.sum(jnp.sum(same, axis=0), axis=0, keepdims=True)
            scales.append(1.0 / jnp.sqrt(acc / (pixels * total) + 1e-06))
        scale = jnp.concatenate(scales, axis=1) * live
    scale_out[...] = jnp.broadcast_to(scale, scale_out.shape)

    put.wait()
    for c in range(CHUNKS):
        run(1, n_py, lambda k: gather_copy(c, k).wait_send())
        run(1, n_px, lambda k: x_copy(c, k).wait_send())
    for step in range(ITERS):
        pltpu.make_async_copy(t_recv.at[step], t_recv.at[step], t_ssem.at[step]).wait()


def per_device(n_py, n_px, movie, traces, footprints, block_ids):
    rows, cols, frames = movie.shape
    pixels = rows * cols
    width = footprints.shape[-1]
    slots = block_ids.shape[-1]
    blk = width // slots
    wid = traces.shape[1]
    loc = traces.shape[0] // blk
    total = n_py * n_px
    hbm = pl.BlockSpec(memory_space=pl.ANY)
    dma = pltpu.SemaphoreType.DMA
    current, scale = pl.pallas_call(
        functools.partial(kernel, n_py, n_px),
        out_shape=(
            jax.ShapeDtypeStruct((pixels, width), F32),
            jax.ShapeDtypeStruct((8, width), F32),
        ),
        in_specs=[hbm, hbm, hbm, pl.BlockSpec(memory_space=pltpu.SMEM)],
        out_specs=(hbm, pl.BlockSpec(memory_space=pltpu.VMEM)),
        scratch_shapes=[
            pltpu.VMEM((pixels, frames), BF),
            pltpu.VMEM((n_px, slots, blk, wid), BF),
            pltpu.VMEM((slots, blk, frames), BF),
            pltpu.VMEM((8, 128) if wid % 128 == 0 else (n_px, slots, blk, wid), BF),
            pltpu.VMEM((pixels, width), F32),
            pltpu.VMEM((pixels, width), F32),
            pltpu.VMEM((slots, width, 2 * blk), BF),
            pltpu.VMEM((8, blk), jnp.int32),
            pltpu.VMEM((n_px, 8, blk), jnp.int32),
            pltpu.SMEM((n_px, 8, blk), jnp.int32),
            pltpu.VMEM((ITERS, 8, blk), F32),
            pltpu.VMEM((ITERS, total - 1, 8, blk), F32),
            pltpu.VMEM((1, width), F32),
            dma((5,)), dma((CHUNKS,)),
            dma((n_px,)), dma((n_px,)),
            dma((CHUNKS, n_py)), dma((CHUNKS, n_py)),
            dma((CHUNKS, n_px)), dma((CHUNKS, n_px)),
            dma((ITERS,)), dma((ITERS,)),
            *[pltpu.VMEM((loc * n_py, blk // CHUNKS, wid), BF) for _ in range(CHUNKS)],
        ],
        compiler_params=pltpu.CompilerParams(
            collective_id=0, has_side_effects=True, vmem_limit_bytes=48 * 1024 * 1024
        ),
    )(
        movie.reshape(pixels, frames),
        traces.reshape(loc, blk, wid),
        footprints.reshape(pixels, width),
        block_ids,
    )
    return (current * scale[:1]).reshape(rows, cols, width)


def solution(mesh):
    return jax.shard_map(
        functools.partial(per_device, mesh.shape["py"], mesh.shape["px"]),
        mesh=mesh,
        in_specs=(P("py", "px", None), P("py", "px"), P("py", "px", None), P("py", "px", None)),
        out_specs=P("py", "px", None),
        check_vma=False,
    )
```

time: 234 us -> 89.4 us (0.38)
  blocking collectives: 93.2 us -> 0 us
  Pallas kernels: 0 us -> 84.4 us
  waiting for transfers between devices: 70.7 us -> 0 us
  matrix products: 27.9 us -> 0 us
  local copies, waits for them, and re-layouts: 17 us -> 3.29 us
  between operations: 13.6 us -> 0.02 us
  starting transfers between devices: 4.74 us -> 0 us
  other arithmetic: 5.86 us -> 1.56 us
    pallas_call x0 -> x1, Pallas kernels: none -> 84.4 us  [per_device(): pl.pallas_call(functools.partial(kernel, n_py, n_px), out_shape=(jax.Shap...]
    psum x2 -> x0, blocking collectives: 79.5 us -> none  [per_device(): totals = lax.psum(partial_value, ('py', 'px'))]
    all_to_all x1 -> x0, waiting for transfers between devices: 43.9 us -> none  [per_device(): lax.all_to_all(outgoing, 'px', split_axis=0, concat_axis=2, tiled=True)]
    dot_general x15 -> x0, matrix products: 27.9 us -> none  [the longest x8 15.4 us: per_device(): jnp.dot(current, gram[:, low:low + BLK], precision=lax.Precision.HIGHEST)]
    all_gather x1 -> x0, waiting for transfers between devices: 26.1 us -> none  [per_device(): span_all = lax.all_gather(traces, 'py', axis=0, tiled=True)]
    all_gather x1 -> x0, blocking collectives: 13.6 us -> none  [per_device(): lax.all_gather(block_ids, 'px', axis=1, tiled=True).reshape(-1, SLOTS)]
    all_to_all x1 -> x0, starting transfers between devices: 4.74 us -> none  [per_device(): lax.all_to_all(outgoing, 'px', split_axis=0, concat_axis=2, tiled=True)]
    gather x1 -> x0, local copies, waits for them, and re-layouts: 4.52 us -> none  [per_device(): denom = jnp.diagonal(gram) + 1e-06 + (1.0 - column_live)]
  transfers between devices with their start and end apart: 2 -> 0, of which waited for: 2 -> 0; matrix products, arithmetic and copies ran while one was open for 2% -> 0% of each run, Pallas kernels for 0% -> 0%
where the time goes in v1:
time: 89.4 us; the launch traced here: 89.2 us
  Pallas kernels  84.4 us (94%)
  local copies, waits for them, and re-layouts  3.29 us (4%)
  other arithmetic  1.56 us (2%)
    pallas_call x1, Pallas kernels, per_device(): pl.pallas_call(functools.partial(kernel, n_py, n_px), out_shape=(jax.Shap...  84.4 us
    unnamed x6, local copies, waits for them, and re-layouts  3.29 us

profile of v1, /device:TPU:0, one launch (start us, length us, event | category | flops | bytes accessed | tf_op | source)
XLA Modules:
  0.0 89.2 jit_solution(9388734006633940239)
XLA Ops:
  0.0 0.0 copy-start
  0.0 1.6 %copy-done = f32[64,16,512]{2,1,0:T(8,128)S(1)} copy-done((f32[64,16,512]{2,1,0:T(8,128)S(1)}, f32[64,16,512]{2,1,0:T(8,128)}, u32[]{:S(2)}) %copy-start) | copy-done | bytes 2097176
  1.6 0.0 copy-start.1
  1.6 1.0 %copy-done.1 = bf16[1024,256]{1,0:T(8,128)(2,1)S(1)} copy-done((bf16[1024,256]{1,0:T(8,128)(2,1)S(1)}, bf16[1024,256]{1,0:T(8,128)(2,1)}, u32[]{:S(2)}) %copy-start.1) | copy-done | bytes 524312
  2.6 0.0 copy-start.2
  2.6 0.7 copy-done.2
  3.3 84.4 %shard_map.46 = (f32[1024,512]{1,0:T(8,128)S(1)}, f32[8,512]{1,0:T(8,128)S(1)}) custom-call(bf16[1024,2048]{1,0:T(8,128)(2,1)} %bitcast.7, bf16[8,128,256]{2,1,0:T(8,128)(2,1)S(1)} %bitcast.6, f32[1024,512]{1,0:T(8,128)S(1)} %bitcast.5, s32[1,1,4]{2,1,0:T(1,128)S(1)} %copy-done.2), custom_call_target="tpu_custom_call" | custom-call | tf_op jit(solution)/shard_map/pallas_call | solution.py:247
  87.7 1.6 %broadcast_multiply_fusion = f32[1024,512]{1,0:T(8,128)} fusion(f32[1024,512]{1,0:T(8,128)S(1)} %get-tuple-element.7, f32[512]{0:T(512)S(1)} %bitcast.8), kind=kLoop, calls=%fused_computation | loop fusion | flops 524288 | bytes 4196352 | tf_op jit(solution)/shard_map/mul | solution.py:285
  (1 shorter events, 0.0 us)
Async XLA Ops:
  0.0 1.6 %copy-start = (f32[64,16,512]{2,1,0:T(8,128)S(1)}, f32[64,16,512]{2,1,0:T(8,128)}, u32[]{:S(2)}) copy-start(f32[64,16,512]{2,1,0:T(8,128)} %param.6) | copy-start | bytes 6291460
  1.6 1.0 %copy-start.1 = (bf16[1024,256]{1,0:T(8,128)(2,1)S(1)}, bf16[1024,256]{1,0:T(8,128)(2,1)}, u32[]{:S(2)}) copy-start(bf16[1024,256]{1,0:T(8,128)(2,1)} %param.5) | copy-start | bytes 1572868
  2.6 0.7 copy-start.2

commit v2 on v1

--- a/solution.py
+++ b/solution.py
@@ -8,7 +8,7 @@
 from jax.sharding import PartitionSpec as P
 
 ITERS = 2
-CHUNKS = 4
+CHUNKS = 8
 MESH = pl.DeviceIdType.MESH
 BF = jnp.bfloat16
 F32 = jnp.float32
@@ -86,15 +86,22 @@
             device_id={"py": lax.rem(py + k, n_py)}, device_id_type=MESH,
         )
 
+    half = CHUNKS // 2
+    pair = max(slots // 2, 1)
+    pieces = [(c, 1, 0, slots) for c in range(half)]
+    pieces += [(half, CHUNKS - half, s, pair) for s in range(0, slots, pair)]
+
     def x_copy(c, k):
-        rows = pl.ds(c * step_rows, step_rows)
+        first, count, low, many = pieces[c]
+        rows = pl.ds(first * step_rows, count * step_rows)
+        group = pl.ds(low, many)
         dest = lax.rem(px + k, n_px)
         if direct:
-            target = recv.at[:, rows, pl.ds(pl.multiple_of(px * wid, wid), wid)]
+            target = recv.at[group, rows, pl.ds(pl.multiple_of(px * wid, wid), wid)]
         else:
-            target = land.at[px, :, rows, :]
+            target = land.at[px, group, rows, :]
         return pltpu.make_async_remote_copy(
-            src_ref=outb.at[dest, :, rows, :],
+            src_ref=outb.at[dest, group, rows, :],
             dst_ref=target,
             send_sem=x_ssem.at[c, k], recv_sem=x_rsem.at[c, k],
             device_id={"px": dest}, device_id_type=MESH,
@@ -123,56 +130,67 @@
         index = jnp.minimum(jnp.maximum(number, 0), nblk - 1)
         return spans[c][index] * ok
 
-    for c in range(CHUNKS):
-        rows = pl.ds(c * step_rows, step_rows)
-        owns[c].wait()
-        run(1, n_py, lambda k: gather_copy(c, k).wait_recv())
+    for c, (first, count, low, many) in enumerate(pieces):
+        if low == 0:
+            for g in range(first, first + count):
+                owns[g].wait()
+                run(1, n_py, lambda k: gather_copy(g, k).wait_recv())
 
         def route(k):
             dest = lax.rem(px + k, n_px)
-            for s in range(slots):
-                outb[dest, s, rows, :] = pick(dest, s, c)
+            for g in range(first, first + count):
+                for s in range(low, low + many):
+                    outb[dest, s, pl.ds(g * step_rows, step_rows), :] = pick(dest, s, g)
             x_copy(c, k).start()
 
         run(1, n_px, route)
-        for s in range(slots):
-            if direct:
-                recv[s, rows, pl.ds(pl.multiple_of(px * wid, wid), wid)] = pick(px, s, c)
-            else:
-                land[px, s, rows, :] = pick(px, s, c)
+        for g in range(first, first + count):
+            rows = pl.ds(g * step_rows, step_rows)
+            for s in range(low, low + many):
+                if direct:
+                    recv[s, rows, pl.ds(pl.multiple_of(px * wid, wid), wid)] = pick(px, s, g)
+                else:
+                    land[px, s, rows, :] = pick(px, s, g)
 
     get_foot.wait()
     get_movie.wait()
-    for c in range(CHUNKS):
+    live = live_row[...]
+    part = min(pixels, 256)
+    frames = recv.shape[2]
+
+    def cross_part(low, i):
+        at = pl.ds(pl.multiple_of(i * part, part), part)
+        cols = pl.ds(low * blk, pair * blk)
+        crs[at, cols] = lax.dot_general(
+            y_buf[at, :], recv[low : low + pair].reshape(pair * blk, frames), (((1,), (1,)), ((), ())),
+            preferred_element_type=F32,
+        )
+
+    def age(i):
+        at = pl.ds(pl.multiple_of(i * part, part), part)
+        cur[at, :] = cur[at, :] * live
+
+    run(0, pixels // part, age)
+    for c, (first, count, low, many) in enumerate(pieces):
         run(1, n_px, lambda k: x_copy(c, k).wait_recv())
-    if not direct:
-        pack = blk // wid
-        for q in range(n_px // pack):
-            both = [land[q * pack + j] for j in range(pack)]
-            recv[:, :, q * blk : (q + 1) * blk] = jnp.concatenate(both, axis=-1)
+        if c < half:
+            continue
+        if not direct:
+            pack = 128 // wid
+            for q in range(n_px // pack):
+                both = [land[q * pack + j, low : low + many] for j in range(pack)]
+                recv[low : low + many, :, q * 128 : (q + 1) * 128] = jnp.concatenate(both, axis=-1)
+        run(0, pixels // part, lambda i: cross_part(low, i))
 
     mine = recv[...].reshape(width, recv.shape[2])
     gram = lax.dot_general(mine, mine, (((1,), (1,)), ((), ())), preferred_element_type=F32)
     eye = lax.broadcasted_iota(jnp.int32, (width, width), 0) == lax.broadcasted_iota(jnp.int32, (width, width), 1)
-    live = live_row[...]
     denom = jnp.sum(jnp.where(eye, gram, 0.0), axis=0, keepdims=True) + 1e-06 + (1.0 - live)
     inv = 1.0 / denom
     hi, lo = split(jnp.where(eye, 1.0, 0.0) - gram * inv)
     for s in range(slots):
         hilo[s, :, :blk] = hi[:, s * blk : (s + 1) * blk]
         hilo[s, :, blk:] = lo[:, s * blk : (s + 1) * blk]
-    part = min(pixels, 256)
-
-    def cross_part(i):
-        at = pl.ds(pl.multiple_of(i * part, part), part)
-        prod = lax.dot_general(
-            y_buf[at, :], recv[...].reshape(width, recv.shape[2]), (((1,), (1,)), ((), ())), preferred_element_type=F32
-        )
-        crs[at, :] = prod * inv
-        cur[at, :] = cur[at, :] * live
-
-    run(0, pixels // part, cross_part)
-
     def total_copy(step, k):
         dest = lax.rem(me + k, total)
         return pltpu.make_async_remote_copy(
@@ -198,7 +216,7 @@
                 wide = mm(jnp.concatenate(his, axis=1), m)
                 thin = mm(jnp.concatenate(los, axis=1), m[:, :blk])
                 fresh = jnp.maximum(
-                    crs[at, s * blk : (s + 1) * blk] + (wide[:, :blk] + wide[:, blk:] + thin), 0.0
+                    crs[at, s * blk : (s + 1) * blk] * inv[:, s * blk : (s + 1) * blk] + (wide[:, :blk] + wide[:, blk:] + thin), 0.0
                 )
                 cur[at, s * blk : (s + 1) * blk] = fresh
                 his[s], los[s] = split(fresh)
@@ -228,6 +246,7 @@
     put.wait()
     for c in range(CHUNKS):
         run(1, n_py, lambda k: gather_copy(c, k).wait_send())
+    for c in range(len(pieces)):
         run(1, n_px, lambda k: x_copy(c, k).wait_send())
     for step in range(ITERS):
         pltpu.make_async_copy(t_recv.at[step], t_recv.at[step], t_ssem.at[step]).wait()
@@ -274,7 +293,7 @@
             *[pltpu.VMEM((loc * n_py, blk // CHUNKS, wid), BF) for _ in range(CHUNKS)],
         ],
         compiler_params=pltpu.CompilerParams(
-            collective_id=0, has_side_effects=True, vmem_limit_bytes=48 * 1024 * 1024
+            collective_id=0, has_side_effects=True, vmem_limit_bytes=67043328
         ),
     )(
         movie.reshape(pixels, frames),

time: 89.4 us -> 87.3 us (0.977)
  local copies, waits for them, and re-layouts: 3.29 us -> 0.72 us
  other arithmetic: 1.56 us -> 3.16 us
  Pallas kernels: 84.4 us -> 83.1 us
    unnamed x6 -> x0, local copies, waits for them, and re-layouts: 3.29 us -> none
    mul x1, other arithmetic: 1.56 us -> 3.16 us  [per_device(): return (current * scale[:1]).reshape(rows, cols, width)]
    pallas_call x1, Pallas kernels: 84.4 us -> 83.1 us  [per_device(): pl.pallas_call(functools.partial(kernel, n_py, n_px), out_shape=(jax.Shap...]
where the time goes in v2:
time: 87.3 us; the launch traced here: 87 us
  Pallas kernels  83.1 us (95%)
  other arithmetic  3.16 us (4%)
    pallas_call x1, Pallas kernels, per_device(): pl.pallas_call(functools.partial(kernel, n_py, n_px), out_shape=(jax.Shap...  83.1 us
    mul x1, other arithmetic, per_device(): return (current * scale[:1]).reshape(rows, cols, width)  3.16 us

profile of v2, /device:TPU:0, one launch (start us, length us, event | category | flops | bytes accessed | tf_op | source)
XLA Modules:
  0.0 87.0 jit_solution(7620978277771154439)
XLA Ops:
  0.0 83.1 %shard_map.46 = (f32[1024,512]{1,0:T(8,128)}, f32[8,512]{1,0:T(8,128)}) custom-call(bf16[1024,2048]{1,0:T(8,128)(2,1)} %bitcast.5, bf16[8,128,256]{2,1,0:T(8,128)(2,1)} %bitcast.7, f32[1024,512]{1,0:T(8,128)} %bitcast.6, s32[1,1,4]{2,1,0:T(1,128)} %ids.1), custom_call_target="tpu_custom_call" | custom-call | tf_op jit(solution)/shard_map/pallas_call | solution.py:266
  83.1 0.7 slice.3
  83.9 3.2 %broadcast_multiply_fusion = f32[1024,512]{1,0:T(8,128)} fusion(f32[1024,512]{1,0:T(8,128)} %get-tuple-element.7, f32[512]{0:T(512)S(1)} %bitcast.8), kind=kLoop, calls=%fused_computation | loop fusion | flops 524288 | bytes 4196352 | tf_op jit(solution)/shard_map/mul | solution.py:304

commit v3 on v2

--- a/solution.py
+++ b/solution.py
@@ -25,7 +25,7 @@
 
 def kernel(
     n_py, n_px, movie, traces, foot, ids, cur_out, scale_out,
-    y_buf, outb, recv, land, cur, crs, hilo, id_tile, id_all, id_smem, t_send, t_recv, live_row,
+    y_buf, outb, recv, land, cur, crs, hilo, id_tile, id_all, id_smem, t_send, t_recv, live_row, gram_buf,
     local_sem, own_sem, id_ssem, id_rsem, g_ssem, g_rsem, x_ssem, x_rsem, t_ssem, t_rsem, *spans,
 ):
     py, px = lax.axis_index("py"), lax.axis_index("px")
@@ -181,9 +181,17 @@
                 both = [land[q * pack + j, low : low + many] for j in range(pack)]
                 recv[low : low + many, :, q * 128 : (q + 1) * 128] = jnp.concatenate(both, axis=-1)
         run(0, pixels // part, lambda i: cross_part(low, i))
-
-    mine = recv[...].reshape(width, recv.shape[2])
-    gram = lax.dot_general(mine, mine, (((1,), (1,)), ((), ())), preferred_element_type=F32)
+        near = slice(low * blk, (low + many) * blk)
+        far = slice(0, (low + many) * blk)
+        fresh_rows = lax.dot_general(
+            recv[low : low + many].reshape(many * blk, frames), recv[: low + many].reshape((low + many) * blk, frames),
+            (((1,), (1,)), ((), ())), preferred_element_type=F32,
+        )
+        gram_buf[near, far] = fresh_rows
+        if low:
+            gram_buf[: low * blk, near] = fresh_rows[:, : low * blk].T
+
+    gram = gram_buf[...]
     eye = lax.broadcasted_iota(jnp.int32, (width, width), 0) == lax.broadcasted_iota(jnp.int32, (width, width), 1)
     denom = jnp.sum(jnp.where(eye, gram, 0.0), axis=0, keepdims=True) + 1e-06 + (1.0 - live)
     inv = 1.0 / denom
@@ -269,7 +277,7 @@
             jax.ShapeDtypeStruct((pixels, width), F32),
             jax.ShapeDtypeStruct((8, width), F32),
         ),
-        in_specs=[hbm, hbm, hbm, pl.BlockSpec(memory_space=pltpu.SMEM)],
+        in_specs=[pl.BlockSpec(memory_space=pltpu.HBM)] * 3 + [pl.BlockSpec(memory_space=pltpu.SMEM)],
         out_specs=(hbm, pl.BlockSpec(memory_space=pltpu.VMEM)),
         scratch_shapes=[
             pltpu.VMEM((pixels, frames), BF),
@@ -285,6 +293,7 @@
             pltpu.VMEM((ITERS, 8, blk), F32),
             pltpu.VMEM((ITERS, total - 1, 8, blk), F32),
             pltpu.VMEM((1, width), F32),
+            pltpu.VMEM((width, width), F32),
             dma((5,)), dma((CHUNKS,)),
             dma((n_px,)), dma((n_px,)),
             dma((CHUNKS, n_py)), dma((CHUNKS, n_py)),
@@ -293,7 +302,7 @@
             *[pltpu.VMEM((loc * n_py, blk // CHUNKS, wid), BF) for _ in range(CHUNKS)],
         ],
         compiler_params=pltpu.CompilerParams(
-            collective_id=0, has_side_effects=True, vmem_limit_bytes=67043328
+            collective_id=0, has_side_effects=True, vmem_limit_bytes=48 * 1024 * 1024
         ),
     )(
         movie.reshape(pixels, frames),

time: 87.3 us -> 86.5 us (level)
  local copies, waits for them, and re-layouts: 0.72 us -> 3.29 us
  other arithmetic: 3.16 us -> 1.56 us
  Pallas kernels: 83.1 us -> 81.5 us
    unnamed x0 -> x6, local copies, waits for them, and re-layouts: none -> 3.29 us
    pallas_call x1, Pallas kernels: 83.1 us -> 81.5 us  [per_device(): pl.pallas_call(functools.partial(kernel, n_py, n_px), out_shape=(jax.Shap...]
    mul x1, other arithmetic: 3.16 us -> 1.56 us  [per_device(): return (current * scale[:1]).reshape(rows, cols, width)]
where the time goes in v3:
time: 86.5 us; the launch traced here: 86.3 us
  Pallas kernels  81.5 us (94%)
  local copies, waits for them, and re-layouts  3.29 us (4%)
  other arithmetic  1.56 us (2%)
    pallas_call x1, Pallas kernels, per_device(): pl.pallas_call(functools.partial(kernel, n_py, n_px), out_shape=(jax.Shap...  81.5 us
    unnamed x6, local copies, waits for them, and re-layouts  3.29 us

profile of v3, /device:TPU:0, one launch (start us, length us, event | category | flops | bytes accessed | tf_op | source)
XLA Modules:
  0.0 86.3 jit_solution(15784345961534371924)
XLA Ops:
  0.0 0.0 copy-start
  0.0 1.6 %copy-done = f32[64,16,512]{2,1,0:T(8,128)S(1)} copy-done((f32[64,16,512]{2,1,0:T(8,128)S(1)}, f32[64,16,512]{2,1,0:T(8,128)}, u32[]{:S(2)}) %copy-start) | copy-done | bytes 2097176
  1.6 0.0 copy-start.1
  1.6 1.0 %copy-done.1 = bf16[1024,256]{1,0:T(8,128)(2,1)S(1)} copy-done((bf16[1024,256]{1,0:T(8,128)(2,1)S(1)}, bf16[1024,256]{1,0:T(8,128)(2,1)}, u32[]{:S(2)}) %copy-start.1) | copy-done | bytes 524312
  2.6 0.0 copy-start.2
  2.6 0.7 copy-done.2
  3.3 81.5 %shard_map.46 = (f32[1024,512]{1,0:T(8,128)S(1)}, f32[8,512]{1,0:T(8,128)S(1)}) custom-call(bf16[1024,2048]{1,0:T(8,128)(2,1)} %bitcast.7, bf16[8,128,256]{2,1,0:T(8,128)(2,1)S(1)} %bitcast.6, f32[1024,512]{1,0:T(8,128)S(1)} %bitcast.5, s32[1,1,4]{2,1,0:T(1,128)S(1)} %copy-done.2), custom_call_target="tpu_custom_call" | custom-call | tf_op jit(solution)/shard_map/pallas_call | solution.py:274
  84.8 1.6 %broadcast_multiply_fusion = f32[1024,512]{1,0:T(8,128)} fusion(f32[1024,512]{1,0:T(8,128)S(1)} %get-tuple-element.7, f32[512]{0:T(512)S(1)} %bitcast.8), kind=kLoop, calls=%fused_computation | loop fusion | flops 524288 | bytes 4196352 | tf_op jit(solution)/shard_map/mul | solution.py:313
  (1 shorter events, 0.0 us)
Async XLA Ops:
  0.0 1.6 %copy-start = (f32[64,16,512]{2,1,0:T(8,128)S(1)}, f32[64,16,512]{2,1,0:T(8,128)}, u32[]{:S(2)}) copy-start(f32[64,16,512]{2,1,0:T(8,128)} %param.6) | copy-start | bytes 6291460
  1.6 1.0 %copy-start.1 = (bf16[1024,256]{1,0:T(8,128)(2,1)S(1)}, bf16[1024,256]{1,0:T(8,128)(2,1)}, u32[]{:S(2)}) copy-start(bf16[1024,256]{1,0:T(8,128)(2,1)} %param.5) | copy-start | bytes 1572868
  2.6 0.7 copy-start.2

commit v4 on v3

--- a/solution.py
+++ b/solution.py
@@ -9,6 +9,7 @@
 
 ITERS = 2
 CHUNKS = 8
+RELAYED = 2
 MESH = pl.DeviceIdType.MESH
 BF = jnp.bfloat16
 F32 = jnp.float32
@@ -23,10 +24,15 @@
     return lax.dot_general(a, b, (((1,), (0,)), ((), ())), preferred_element_type=F32)
 
 
+def relayed(n_py, n_px, wid):
+    return RELAYED if wid % 128 == 0 and n_px == 2 * n_py and n_py > 2 else 0
+
+
 def kernel(
     n_py, n_px, movie, traces, foot, ids, cur_out, scale_out,
     y_buf, outb, recv, land, cur, crs, hilo, id_tile, id_all, id_smem, t_send, t_recv, live_row, gram_buf,
-    local_sem, own_sem, id_ssem, id_rsem, g_ssem, g_rsem, x_ssem, x_rsem, t_ssem, t_rsem, *spans,
+    local_sem, own_sem, id_ssem, id_rsem, g_ssem, g_rsem, x_ssem, x_rsem, t_ssem, t_rsem,
+    z_buf, p_buf, outp, idp_all, idp_smem, z_sem, p_ssem, p_rsem, q_ssem, q_rsem, idp_ssem, idp_rsem, *spans,
 ):
     py, px = lax.axis_index("py"), lax.axis_index("px")
     total = n_py * n_px
@@ -38,15 +44,25 @@
     direct = wid % 128 == 0
     pixels = y_buf.shape[0]
     step_rows = blk // CHUNKS
+    relay = relayed(n_py, n_px, wid)
+    chunks = CHUNKS - relay
+    plane = 2 * n_py
+    z, core = px // 2, lax.rem(px, 2)
+    spot = py * 2 + core
+    nz = n_px // 2
+    rest = pl.ds(chunks * step_rows, relay * step_rows)
 
     owns = [
         pltpu.make_async_copy(
             traces.at[:, pl.ds(c * step_rows, step_rows), :], spans[c].at[pl.ds(py * loc, loc)], own_sem.at[c]
         )
-        for c in range(CHUNKS)
+        for c in range(chunks)
     ]
     for own in owns:
         own.start()
+    if relay:
+        own_z = pltpu.make_async_copy(traces.at[:, rest, :], z_buf.at[z], local_sem.at[5])
+        own_z.start()
     get_foot = pltpu.make_async_copy(foot, cur, local_sem.at[1])
     get_movie = pltpu.make_async_copy(movie, y_buf, local_sem.at[2])
 
@@ -56,6 +72,8 @@
         tile = jnp.where(sub == 4 + s, ids[0, 0, s], tile)
     id_tile[...] = tile
     id_all[px] = tile
+    if relay:
+        idp_all[spot] = tile
     for s in range(slots):
         alive = ((tile[4 + s : 5 + s, :] >= 0) & (tile[4 + s : 5 + s, :] < nblk)).astype(F32)
         live_row[:, s * blk : (s + 1) * blk] = alive
@@ -86,10 +104,10 @@
             device_id={"py": lax.rem(py + k, n_py)}, device_id_type=MESH,
         )
 
-    half = CHUNKS // 2
+    half = chunks // 2
     pair = max(slots // 2, 1)
     pieces = [(c, 1, 0, slots) for c in range(half)]
-    pieces += [(half, CHUNKS - half, s, pair) for s in range(0, slots, pair)]
+    pieces += [(half, chunks - half, s, pair) for s in range(0, slots, pair)]
 
     def x_copy(c, k):
         first, count, low, many = pieces[c]
@@ -114,8 +132,60 @@
 
         lax.fori_loop(lo, hi, body, 0)
 
+    def plane_dest(k):
+        other = lax.rem(spot + k, plane)
+        return other, {"py": other // 2, "px": z * 2 + lax.rem(other, 2)}
+
+    def idp_copy(k):
+        return pltpu.make_async_remote_copy(
+            src_ref=id_tile, dst_ref=idp_all.at[spot], send_sem=idp_ssem.at[k], recv_sem=idp_rsem.at[k],
+            device_id=plane_dest(k)[1], device_id_type=MESH,
+        )
+
+    def chain(way, j):
+        source = z - j if way == 0 else z + j
+        return pltpu.make_async_remote_copy(
+            src_ref=z_buf.at[source], dst_ref=z_buf.at[source],
+            send_sem=z_sem.at[way, 0, j], recv_sem=z_sem.at[way, 1, j],
+            device_id={"px": px + 2 if way == 0 else px - 2}, device_id_type=MESH,
+        )
+
+    def chain_sends(way, j):
+        return (z - j >= 0) & (z + 1 < nz) if way == 0 else (z + j < nz) & (z - 1 >= 0)
+
+    def chain_start(j):
+        for way in range(2):
+            pl.when(chain_sends(way, j))(lambda: chain(way, j).start())
+
+    def chain_wait(j):
+        for way in range(2):
+            source = z - 1 - j if way == 0 else z + 1 + j
+            here = source >= 0 if way == 0 else source < nz
+
+            @pl.when(here)
+            def _():
+                pltpu.make_async_copy(z_buf.at[source], z_buf.at[source], z_sem.at[way, 1, j]).wait()
+
+    def p_copy(k):
+        other = lax.rem(py + k, n_py)
+        return pltpu.make_async_remote_copy(
+            src_ref=z_buf.at[other], dst_ref=p_buf.at[pl.ds(py * loc, loc)],
+            send_sem=p_ssem.at[k], recv_sem=p_rsem.at[k], device_id={"py": other}, device_id_type=MESH,
+        )
+
+    def q_copy(k):
+        other, place = plane_dest(k)
+        return pltpu.make_async_remote_copy(
+            src_ref=outp.at[other], dst_ref=recv.at[:, rest, pl.ds(pl.multiple_of(spot * wid, wid), wid)],
+            send_sem=q_ssem.at[k], recv_sem=q_rsem.at[k], device_id=place, device_id_type=MESH,
+        )
+
     run(1, n_px, lambda k: id_copy(k).start())
-    for c in range(CHUNKS):
+    if relay:
+        run(1, plane, lambda k: idp_copy(k).start())
+        own_z.wait()
+        chain_start(0)
+    for c in range(chunks):
         run(1, n_py, lambda k: gather_copy(c, k).start())
     get_movie.start()
     get_foot.start()
@@ -124,13 +194,33 @@
     to_smem.start()
     to_smem.wait()
 
+    if relay:
+        run(1, plane, lambda k: idp_copy(k).wait())
+        to_plane = pltpu.make_async_copy(idp_all, idp_smem, local_sem.at[6])
+        to_plane.start()
+        to_plane.wait()
+
+    def pick_plane(dest, s):
+        number = idp_smem[dest, 4 + s, 0]
+        ok = ((number >= 0) & (number < nblk)).astype(F32).astype(BF)
+        return p_buf[jnp.minimum(jnp.maximum(number, 0), nblk - 1)] * ok
+
     def pick(dest, s, c):
         number = id_smem[dest, 4 + s, 0]
         ok = ((number >= 0) & (number < nblk)).astype(F32).astype(BF)
         index = jnp.minimum(jnp.maximum(number, 0), nblk - 1)
         return spans[c][index] * ok
 
+    own_p = pltpu.make_async_copy(z_buf.at[lax.rem(py, z_buf.shape[0])], p_buf.at[pl.ds(py * loc, loc)], local_sem.at[5])
+    moves = nz - 1 if relay else 0
     for c, (first, count, low, many) in enumerate(pieces):
+        if c < moves:
+            chain_wait(c)
+            if c + 1 < moves:
+                chain_start(c + 1)
+            else:
+                own_p.start()
+                run(1, n_py, lambda k: p_copy(k).start())
         if low == 0:
             for g in range(first, first + count):
                 owns[g].wait()
@@ -152,6 +242,20 @@
                 else:
                     land[px, s, rows, :] = pick(px, s, g)
 
+    if relay:
+        own_p.wait()
+        run(1, n_py, lambda k: p_copy(k).wait_recv())
+
+        def route_plane(k):
+            other = lax.rem(spot + k, plane)
+            for s in range(slots):
+                outp[other, s] = pick_plane(other, s)
+            q_copy(k).start()
+
+        run(1, plane, route_plane)
+        for s in range(slots):
+            recv[s, rest, pl.ds(pl.multiple_of(spot * wid, wid), wid)] = pick_plane(spot, s)
+
     get_foot.wait()
     get_movie.wait()
     live = live_row[...]
@@ -175,6 +279,8 @@
         run(1, n_px, lambda k: x_copy(c, k).wait_recv())
         if c < half:
             continue
+        if relay and low == 0:
+            run(1, plane, lambda k: q_copy(k).wait_recv())
         if not direct:
             pack = 128 // wid
             for q in range(n_px // pack):
@@ -252,8 +358,14 @@
     scale_out[...] = jnp.broadcast_to(scale, scale_out.shape)
 
     put.wait()
-    for c in range(CHUNKS):
+    for c in range(chunks):
         run(1, n_py, lambda k: gather_copy(c, k).wait_send())
+    if relay:
+        for j in range(moves):
+            for way in range(2):
+                pl.when(chain_sends(way, j))(lambda: chain(way, j).wait_send())
+        run(1, n_py, lambda k: p_copy(k).wait_send())
+        run(1, plane, lambda k: q_copy(k).wait_send())
     for c in range(len(pieces)):
         run(1, n_px, lambda k: x_copy(c, k).wait_send())
     for step in range(ITERS):
@@ -269,6 +381,10 @@
     wid = traces.shape[1]
     loc = traces.shape[0] // blk
     total = n_py * n_px
+    relay = relayed(n_py, n_px, wid)
+    part = relay * (blk // CHUNKS) or 16
+    hold = n_py if relay else 1
+    plane = 2 * hold
     hbm = pl.BlockSpec(memory_space=pl.ANY)
     dma = pltpu.SemaphoreType.DMA
     current, scale = pl.pallas_call(
@@ -294,15 +410,24 @@
             pltpu.VMEM((ITERS, total - 1, 8, blk), F32),
             pltpu.VMEM((1, width), F32),
             pltpu.VMEM((width, width), F32),
-            dma((5,)), dma((CHUNKS,)),
+            dma((7,)), dma((CHUNKS,)),
             dma((n_px,)), dma((n_px,)),
             dma((CHUNKS, n_py)), dma((CHUNKS, n_py)),
             dma((CHUNKS, n_px)), dma((CHUNKS, n_px)),
             dma((ITERS,)), dma((ITERS,)),
-            *[pltpu.VMEM((loc * n_py, blk // CHUNKS, wid), BF) for _ in range(CHUNKS)],
+            pltpu.VMEM((hold, loc, part, wid), BF),
+            pltpu.VMEM((loc * n_py, part, wid), BF),
+            pltpu.VMEM((plane, slots, part, wid), BF),
+            pltpu.VMEM((plane, 8, blk), jnp.int32),
+            pltpu.SMEM((plane, 8, blk), jnp.int32),
+            dma((2, 2, n_px)),
+            dma((n_py,)), dma((n_py,)),
+            dma((plane,)), dma((plane,)),
+            dma((plane,)), dma((plane,)),
+            *[pltpu.VMEM((loc * n_py, blk // CHUNKS, wid), BF) for _ in range(CHUNKS - relay)],
         ],
         compiler_params=pltpu.CompilerParams(
-            collective_id=0, has_side_effects=True, vmem_limit_bytes=48 * 1024 * 1024
+            collective_id=0, has_side_effects=True, vmem_limit_bytes=67043328
         ),
     )(
         movie.reshape(pixels, frames),

time: 86.5 us -> 80 us (0.925)
  Pallas kernels: 81.5 us -> 75.8 us
  local copies, waits for them, and re-layouts: 3.29 us -> 0.72 us
  other arithmetic: 1.56 us -> 3.16 us
    pallas_call x1, Pallas kernels: 81.5 us -> 75.8 us  [per_device(): pl.pallas_call(functools.partial(kernel, n_py, n_px), out_shape=(jax.Shap...]
    unnamed x6 -> x0, local copies, waits for them, and re-layouts: 3.29 us -> none
    mul x1, other arithmetic: 1.56 us -> 3.16 us  [per_device(): return (current * scale[:1]).reshape(rows, cols, width)]
where the time goes in v4:
time: 80 us; the launch traced here: 79.7 us
  Pallas kernels  75.8 us (95%)
  other arithmetic  3.16 us (4%)
    pallas_call x1, Pallas kernels, per_device(): pl.pallas_call(functools.partial(kernel, n_py, n_px), out_shape=(jax.Shap...  75.8 us
    mul x1, other arithmetic, per_device(): return (current * scale[:1]).reshape(rows, cols, width)  3.16 us

profile of v4, /device:TPU:0, one launch (start us, length us, event | category | flops | bytes accessed | tf_op | source)
XLA Modules:
  0.0 79.7 jit_solution(10050223536485272023)
XLA Ops:
  0.0 75.8 %shard_map.46 = (f32[1024,512]{1,0:T(8,128)}, f32[8,512]{1,0:T(8,128)}) custom-call(bf16[1024,2048]{1,0:T(8,128)(2,1)} %bitcast.5, bf16[8,128,256]{2,1,0:T(8,128)(2,1)} %bitcast.7, f32[1024,512]{1,0:T(8,128)} %bitcast.6, s32[1,1,4]{2,1,0:T(1,128)} %ids.1), custom_call_target="tpu_custom_call" | custom-call | tf_op jit(solution)/shard_map/pallas_call | solution.py:390
  75.9 0.7 slice.3
  76.6 3.2 %broadcast_multiply_fusion = f32[1024,512]{1,0:T(8,128)} fusion(f32[1024,512]{1,0:T(8,128)} %get-tuple-element.7, f32[512]{0:T(512)S(1)} %bitcast.8), kind=kLoop, calls=%fused_computation | loop fusion | flops 524288 | bytes 4196352 | tf_op jit(solution)/shard_map/mul | solution.py:438

commit v5 on v4

--- a/solution.py
+++ b/solution.py
@@ -9,7 +9,7 @@
 
 ITERS = 2
 CHUNKS = 8
-RELAYED = 2
+RELAYED = 3
 MESH = pl.DeviceIdType.MESH
 BF = jnp.bfloat16
 F32 = jnp.float32

time: 80 us -> 84.1 us (1.051)
  Pallas kernels: 75.8 us -> 80 us
    pallas_call x1, Pallas kernels: 75.8 us -> 80 us  [per_device(): pl.pallas_call(functools.partial(kernel, n_py, n_px), out_shape=(jax.Shap...]
where the time goes in v5:
time: 84.1 us; the launch traced here: 83.9 us
  Pallas kernels  80 us (95%)
  other arithmetic  3.16 us (4%)
    pallas_call x1, Pallas kernels, per_device(): pl.pallas_call(functools.partial(kernel, n_py, n_px), out_shape=(jax.Shap...  80 us
    mul x1, other arithmetic, per_device(): return (current * scale[:1]).reshape(rows, cols, width)  3.16 us

profile of v5, /device:TPU:0, one launch (start us, length us, event | category | flops | bytes accessed | tf_op | source)
XLA Modules:
  0.0 83.9 jit_solution(7825197005277053620)
XLA Ops:
  0.0 80.0 %shard_map.46 = (f32[1024,512]{1,0:T(8,128)}, f32[8,512]{1,0:T(8,128)}) custom-call(bf16[1024,2048]{1,0:T(8,128)(2,1)} %bitcast.5, bf16[8,128,256]{2,1,0:T(8,128)(2,1)} %bitcast.7, f32[1024,512]{1,0:T(8,128)} %bitcast.6, s32[1,1,4]{2,1,0:T(1,128)} %ids.1), custom_call_target="tpu_custom_call" | custom-call | tf_op jit(solution)/shard_map/pallas_call | solution.py:390
  80.0 0.7 slice.3
  80.8 3.2 %broadcast_multiply_fusion = f32[1024,512]{1,0:T(8,128)} fusion(f32[1024,512]{1,0:T(8,128)} %get-tuple-element.7, f32[512]{0:T(512)S(1)} %bitcast.8), kind=kLoop, calls=%fused_computation | loop fusion | flops 524288 | bytes 4196352 | tf_op jit(solution)/shard_map/mul | solution.py:438

commit v6 on v4

--- a/solution.py
+++ b/solution.py
@@ -259,7 +259,7 @@
     get_foot.wait()
     get_movie.wait()
     live = live_row[...]
-    part = min(pixels, 256)
+    part = min(pixels, 512)
     frames = recv.shape[2]
 
     def cross_part(low, i):

time: 80 us -> 77.5 us (0.969)
  Pallas kernels: 75.8 us -> 73.3 us
    pallas_call x1, Pallas kernels: 75.8 us -> 73.3 us  [per_device(): pl.pallas_call(functools.partial(kernel, n_py, n_px), out_shape=(jax.Shap...]
where the time goes in v6:
time: 77.5 us; the launch traced here: 77.2 us
  Pallas kernels  73.3 us (95%)
  other arithmetic  3.16 us (4%)
    pallas_call x1, Pallas kernels, per_device(): pl.pallas_call(functools.partial(kernel, n_py, n_px), out_shape=(jax.Shap...  73.3 us
    mul x1, other arithmetic, per_device(): return (current * scale[:1]).reshape(rows, cols, width)  3.16 us

profile of v6, /device:TPU:0, one launch (start us, length us, event | category | flops | bytes accessed | tf_op | source)
XLA Modules:
  0.0 77.2 jit_solution(524281930759116353)
XLA Ops:
  0.0 73.3 %shard_map.46 = (f32[1024,512]{1,0:T(8,128)}, f32[8,512]{1,0:T(8,128)}) custom-call(bf16[1024,2048]{1,0:T(8,128)(2,1)} %bitcast.5, bf16[8,128,256]{2,1,0:T(8,128)(2,1)} %bitcast.7, f32[1024,512]{1,0:T(8,128)} %bitcast.6, s32[1,1,4]{2,1,0:T(1,128)} %ids.1), custom_call_target="tpu_custom_call" | custom-call | tf_op jit(solution)/shard_map/pallas_call | solution.py:390
  73.3 0.7 slice.3
  74.1 3.2 %broadcast_multiply_fusion = f32[1024,512]{1,0:T(8,128)} fusion(f32[1024,512]{1,0:T(8,128)} %get-tuple-element.7, f32[512]{0:T(512)S(1)} %bitcast.8), kind=kLoop, calls=%fused_computation | loop fusion | flops 524288 | bytes 4196352 | tf_op jit(solution)/shard_map/mul | solution.py:438
